TPU v7x, 32 devices: a whole 2x2x4 slice. The times are simulated.
32 devices in a mesh: groups: 2 (over x), seq: 16 (over z, y, core).
Axes of the slice: x: 2, y: 2, z: 4, core: 2. Of those that a mesh axis runs over, the one named last changes fastest.
Arguments:
- images: bfloat16 [4, 2048, 3072], P('groups', 'seq'), parts along dimension 0, may hold values from -6 to 6
- w_qkv: bfloat16 [3072, 1152], replicated, may hold values from -0.109375 to 0.109375
- b_qkv: float32 [1152], replicated, may hold values from -3 to 3
- q_gain: float32 [128], replicated, may hold values from 0.5 to 2.5
- k_gain: float32 [128], replicated, may hold values from 0.5 to 2.5
- key_basis: float32 [3, 128, 32], replicated, may hold values from -0.5 to 0.5
- value_basis: float32 [3, 128, 32], replicated, may hold values from -0.5 to 0.5
- centers: float32 [4, 2, 3, 128], P('groups'), parts along dimension 0, may hold values from -22 to 22
- refresh: int32 [2, 3], replicated, may hold values 0 or 1
- w_out: bfloat16 [384, 3072], replicated, may hold values from -0.3125 to 0.3125
Outputs:
- mixed: bfloat16 [4, 2048, 3072], P('groups', 'seq'), parts along dimension 0
- new_centers: float32 [4, 2, 3, 128], P('groups'), parts along dimension 0
There are 2 independent parts, one for each index of `groups`. A program takes and returns all parts, laid end to end along the dimension named above; an argument that names none is the same for every part. Nothing has to cross between parts.
All inputs are finite; a program needn't handle non-finite values.
Results may differ from a plain program's by a relative error of at most 0.0051.
Values may be sent and summed in bfloat16 or wider, within the bound.
A program may use at most 64 MiB of HBM per device.

v0:
```python
import math

import jax
import jax.numpy as jnp
from jax import lax
from jax.sharding import PartitionSpec as P

epsilon = 1e-06
highest = lax.Precision.HIGHEST


def normalize(values, gain):
    mean_square = jnp.mean(values * values, axis=-1, keepdims=True)
    return values * lax.rsqrt(mean_square + epsilon) * gain


def per_device(
    images, w_qkv, b_qkv, q_gain, k_gain, key_basis, value_basis, centers, refresh, w_out
):
    sample_count, tokens_dev, model_width = images.shape
    head_count, head_dim, code_rank = key_basis.shape
    seq_count = lax.axis_size("seq")
    first_row = lax.axis_index("seq") * tokens_dev
    factor = 1.0 / math.sqrt(head_dim)
    flat_images = images.reshape(sample_count * tokens_dev, model_width)
    projected = jnp.dot(flat_images, w_qkv, preferred_element_type=jnp.float32) + b_qkv
    projected = projected.reshape(sample_count, tokens_dev, 3, head_count, head_dim)
    queries = normalize(projected[:, :, 0], q_gain)
    keys_local = normalize(projected[:, :, 1], k_gain)
    values_local = projected[:, :, 2]
    key_center = centers[:, 0]
    value_center = centers[:, 1]
    key_codes = jnp.einsum(
        "bthd,hdr->bthr", keys_local - key_center[:, None], key_basis, precision=highest
    ).astype(jnp.bfloat16)
    value_codes = jnp.einsum(
        "bthd,hdr->bthr", values_local - value_center[:, None], value_basis, precision=highest
    ).astype(jnp.bfloat16)
    local_sums = jnp.stack([jnp.sum(keys_local, axis=1), jnp.sum(values_local, axis=1)], axis=1)
    summed = lax.psum(local_sums, "seq")
    fresh_means = summed / (tokens_dev * seq_count)
    new_centers = jnp.where(refresh[None, :, :, None] == 1, fresh_means, centers)
    query_heads = queries.transpose(0, 2, 1, 3)
    key_heads = keys_local.transpose(0, 2, 1, 3)
    value_heads = values_local.transpose(0, 2, 1, 3)
    near_scores = jnp.einsum("bhqd,bhsd->bhqs", query_heads, key_heads, precision=highest) * factor
    start_max = jnp.max(near_scores, axis=-1)
    near_weights = jnp.exp(near_scores - start_max[..., None])
    start_sum = jnp.sum(near_weights, axis=-1)
    start_weighted = jnp.einsum("bhqs,bhsd->bhqd", near_weights, value_heads, precision=highest)
    packed = jnp.stack([key_codes, value_codes], axis=2)
    packed = packed.transpose(1, 0, 2, 3, 4).reshape(
        tokens_dev, sample_count, 2 * head_count * code_rank
    )

    def absorb(running, code_block, owned, low_sample, high_sample):
        row_max, row_sum, weighted = running
        block_values = code_block.astype(jnp.float32)
        key_part = block_values[:, :, 0]
        value_part = block_values[:, :, 1]
        key_rebuilt = (
            jnp.einsum("sbhr,hdr->bhsd", key_part, key_basis, precision=highest)
            + key_center[low_sample:high_sample, :, None, :]
        )
        scores = jnp.einsum("bhqd,bhsd->bhqs", query_heads, key_rebuilt, precision=highest) * factor
        scores = jnp.where(owned[None, None, None, :], -jnp.inf, scores)
        new_max = jnp.maximum(row_max, jnp.max(scores, axis=-1))
        fading = jnp.exp(row_max - new_max)
        weights = jnp.exp(scores - new_max[..., None])
        weight_sum = jnp.sum(weights, axis=-1)
        value_rebuilt = (
            jnp.einsum("sbhr,hdr->bhsd", value_part, value_basis, precision=highest)
            + value_center[low_sample:high_sample, :, None, :]
        )
        addition = jnp.einsum("bhqs,bhsd->bhqd", weights, value_rebuilt, precision=highest)
        return (new_max, row_sum * fading + weight_sum, weighted * fading[..., None] + addition)

    start_state = (start_max, start_sum, start_weighted)
    whole_codes = packed.reshape(tokens_dev, sample_count * 2 * head_count * code_rank)
    shard_codes = lax.all_gather(whole_codes, "seq", axis=0, tiled=True)
    row_count = shard_codes.shape[0]
    code_block = shard_codes.reshape(row_count, sample_count - 0, 2, head_count, code_rank)
    positions = jnp.arange(row_count, dtype=jnp.int32)
    owned = (positions >= first_row) & (positions < first_row + tokens_dev)
    block_rows = 512
    block_count = row_count // block_rows

    def advance(inner, blocks):
        return (absorb(inner, blocks[0], blocks[1], 0, sample_count), None)

    stacked = (
        code_block.reshape(block_count, block_rows, sample_count - 0, 2, head_count, code_rank),
        owned.reshape(block_count, block_rows),
    )
    result, unused = lax.scan(advance, start_state, stacked)
    final_max, final_sum, final_weighted = result
    attended = (final_weighted / final_sum[..., None]).transpose(0, 2, 1, 3)
    attended = attended.reshape(sample_count * tokens_dev, head_count * head_dim).astype(
        jnp.bfloat16
    )
    mixed = jnp.dot(attended, w_out, preferred_element_type=jnp.float32).astype(jnp.bfloat16)
    return (mixed.reshape(sample_count, tokens_dev, model_width), new_centers)


def solution(mesh):
    return jax.shard_map(
        per_device,
        mesh=mesh,
        in_specs=(
            P("groups", "seq", None),
            P(),
            P(),
            P(),
            P(),
            P(),
            P(),
            P("groups", None, None, None),
            P(),
            P(),
        ),
        out_specs=(P("groups", "seq", None), P("groups", None, None, None)),
        check_vma=False,
    )
```

profile of v0, /device:TPU:0, one launch (start us, length us, event | category | flops | bytes accessed | tf_op | source)
XLA Modules:
  0.0 120.0 jit_solution(16905698591683552414)
XLA Ops:
  7.2 5.8 %convolution_add_fusion = f32[256,1152]{1,0:T(8,128)S(1)} fusion(bf16[256,3072]{1,0:T(8,128)(2,1)} %bitcast.143, bf16[3072,1152]{1,0:T(8,128)(2,1)} %param.13, f32[1152]{0:T(1024)} %param.14), kind=kOutput, calls=%fused_computation.24 | convolution fusion | flops 1812234240 | bytes 9835008 | tf_op jit(solution)/shard_map/dot_general | solution.py:26
  13.0 1.4 %copy.42 = f32[256,1152]{0,1:T(8,128)} copy(f32[256,1152]{1,0:T(8,128)S(1)} %convolution_add_fusion) | data formatting | bytes 2359296 | tf_op jit(solution)/shard_map/add | solution.py:26
  14.4 1.9 %reshape.48 = f32[2,128,3,3,128]{1,0,4,3,2:T(2,128)S(1)} reshape(f32[256,1152]{0,1:T(8,128)} %copy.42) | data formatting | bytes 2359296 | tf_op jit(solution)/shard_map/reshape | solution.py:27
  17.2 1.8 %slice_reduce_fusion = (f32[2,3,128]{0,2,1:T(8,128)}, f32[2,128,1,3,128]{1,0,4,3,2:T(2,128)}) fusion(f32[2,128,3,3,128]{1,0,4,3,2:T(2,128)S(1)} %reshape.48), kind=kLoop, calls=%fused_computation.64 | loop fusion | flops 97536 | bytes 789504 | tf_op jit(solution)/shard_map/reduce_sum | solution.py:39
  18.9 1.9 %copy.64 = f32[2,128,1,3,128]{4,1,3,0,2:T(8,128)} copy(f32[2,128,1,3,128]{1,0,4,3,2:T(2,128)} %get-tuple-element.119) | data formatting | bytes 786432
  22.5 2.6 %fusion.32 = (f32[2,3,128]{0,2,1:T(8,128)}, f32[2,128,3,128]{1,0,3,2:T(2,128)S(1)}, f32[2,3,128,128]{2,0,3,1:T(2,128)}) fusion(f32[128]{0:T(128)} %param.16, f32[2,128,3]{1,0,2:T(2,128)S(1)} %get-tuple-element.129, f32[2,128,3,3,128]{1,0,4,3,2:T(2,128)S(1)} %reshape.48, f32[128]{0:T(128)} %param.15, f32[2,128,3]{1,0,2:T(2,128)S(1)} %get-tuple-element.130), kind=kLoop, calls=%fused_computation.65 | loop fusion | flops 490752 | bytes 1583104 | tf_op jit(solution)/shard_map/reduce_sum | solution.py:39
  27.1 1.2 copy.43
  28.3 1.6 %copy.56 = f32[2,3,128]{2,0,1:T(2,128)} copy(f32[2,3,128]{0,2,1:T(8,128)} %get-tuple-element.114) | data formatting | bytes 6144 | tf_op jit(solution)/shard_map/reduce_sum | solution.py:39
  29.9 1.6 %copy.57 = f32[2,3,128]{2,0,1:T(2,128)} copy(f32[2,3,128]{0,2,1:T(8,128)} %get-tuple-element.118) | data formatting | bytes 6144 | tf_op jit(solution)/shard_map/reduce_sum | solution.py:39
  32.2 36.5 %psum.7 = f32[2,2,3,128]{3,0,2,1:T(2,128)} all-reduce(f32[2,2,3,128]{3,0,2,1:T(2,128)S(1)} %pad_maximum_fusion), channel_id=1, replica_groups=mesh['groups'=2,'seq'=16] {'seq'}, use_global_device_ids=true, to_apply=%region_10.11 | all-reduce | flops 1536 | bytes 12288 | tf_op jit(solution)/shard_map/psum | solution.py:40
  73.2 3.9 %reshape_reshape.7 = bf16[4,512,2,2,3,32]{1,0,5,4,3,2:T(4,128)(2,1)} reshape(bf16[2048,384]{0,1:T(8,128)(2,1)} %all-gather.2.cloned.1.call-done) | data formatting | bytes 3145728 | tf_op jit(solution)/shard_map/reshape;reshape | solution.py:92
  77.0 2.9 %copy.53 = bf16[4,512,2,2,3,32]{1,5,4,2,3,0:T(8,128)(2,1)} copy(bf16[4,512,2,2,3,32]{1,0,5,4,3,2:T(4,128)(2,1)} %reshape_reshape.7) | data formatting | bytes 3145728 | tf_op jit(solution)/shard_map/while | solution.py:95
  80.0 30.7 %while.14 = (s32[]{:T(128)}, f32[2,3,128]{2,1,0:T(4,128)S(1)}, f32[2,3,128]{2,1,0:T(4,128)S(1)}, f32[2,3,128,128]{3,2,1,0:T(8,128)S(1)}, pred[4,512]{1,0:T(4,128...) while((s32[]{:T(128)}, f32[2,3,128]{2,1,0:T(4,128)S(1)}, ...), condition=%wide.region_7.8_spmd, body=%wide.region_4.7_spmd.sunk | while | flops 1513293312 | bytes 13524605 | solution.py:95
  80.0 1.0 dynamic-slice_bitcast_fusion.2
  81.9 1.6 %bitcast_reduce_fusion.2 = (f32[2,3,128]{2,1,0:T(4,128)S(1)}, f32[2,3,512,128]{3,2,1,0:T(8,128)S(1)}) fusion(f32[2,3,128,128]{3,2,1,0:T(8,128)S(1)} %get-tuple-element.240, f32[3,512,2,128]{3,1,0,2:T(8,128)S(1)} %fusion.54, f32[2,3,128]{2,1,0:T(4,128)S(1)} %bitcast.140, pred[512]{0:T(512)(128)(4,1)S(1)} %dynamic-slice_reduce_fusion.2), kind=kOutput, calls=%fused_computation.3.clone.1 | convolution fusion | flops 605551872 | bytes 3545600 | tf_op jit(solution)/shard_map/while/body/eval_jaxpr/bhqd,bhsd->bhqs/dot_general | solution.py:65
  84.8 2.9 %fusion.57 = f32[2,3,128,128]{3,2,1,0:T(8,128)S(1)} fusion(f32[3,512,2,128]{3,1,0,2:T(8,128)S(1)} %fusion.56, f32[2,3,512,128]{3,2,1,0:T(8,128)S(1)} %get-tuple-element.205, f32[2,3,128]{2,1,0:T(4,128)S(1)} %bitcast.139, f32[2,3,128]{2,1,0:T(4,128)S(1)} %max.4, f32[2,3,128,128]{3,2,1,0:T(8,128)S(1)} %get-tuple-element.223, ...), kind=kOutput, calls=%fused_computation.9.clone.1 | convolution fusion | flops 604962816 | bytes 3941376 | tf_op jit(solution)/shard_map/while/body/eval_jaxpr/bhqs,bhsd->bhqd/dot_general | solution.py:75
  87.7 1.0 dynamic-slice_bitcast_fusion.2
  89.6 1.6 %bitcast_reduce_fusion.2 = (f32[2,3,128]{2,1,0:T(4,128)S(1)}, f32[2,3,512,128]{3,2,1,0:T(8,128)S(1)}) fusion(f32[2,3,128,128]{3,2,1,0:T(8,128)S(1)} %get-tuple-element.240, f32[3,512,2,128]{3,1,0,2:T(8,128)S(1)} %fusion.54, f32[2,3,128]{2,1,0:T(4,128)S(1)} %bitcast.140, pred[512]{0:T(512)(128)(4,1)S(1)} %dynamic-slice_reduce_fusion.2), kind=kOutput, calls=%fused_computation.3.clone.1 | convolution fusion | flops 605551872 | bytes 3545600 | tf_op jit(solution)/shard_map/while/body/eval_jaxpr/bhqd,bhsd->bhqs/dot_general | solution.py:65
  92.4 2.9 %fusion.57 = f32[2,3,128,128]{3,2,1,0:T(8,128)S(1)} fusion(f32[3,512,2,128]{3,1,0,2:T(8,128)S(1)} %fusion.56, f32[2,3,512,128]{3,2,1,0:T(8,128)S(1)} %get-tuple-element.205, f32[2,3,128]{2,1,0:T(4,128)S(1)} %bitcast.139, f32[2,3,128]{2,1,0:T(4,128)S(1)} %max.4, f32[2,3,128,128]{3,2,1,0:T(8,128)S(1)} %get-tuple-element.223, ...), kind=kOutput, calls=%fused_computation.9.clone.1 | convolution fusion | flops 604962816 | bytes 3941376 | tf_op jit(solution)/shard_map/while/body/eval_jaxpr/bhqs,bhsd->bhqd/dot_general | solution.py:75
  97.3 1.6 %bitcast_reduce_fusion.2 = (f32[2,3,128]{2,1,0:T(4,128)S(1)}, f32[2,3,512,128]{3,2,1,0:T(8,128)S(1)}) fusion(f32[2,3,128,128]{3,2,1,0:T(8,128)S(1)} %get-tuple-element.240, f32[3,512,2,128]{3,1,0,2:T(8,128)S(1)} %fusion.54, f32[2,3,128]{2,1,0:T(4,128)S(1)} %bitcast.140, pred[512]{0:T(512)(128)(4,1)S(1)} %dynamic-slice_reduce_fusion.2), kind=kOutput, calls=%fused_computation.3.clone.1 | convolution fusion | flops 605551872 | bytes 3545600 | tf_op jit(solution)/shard_map/while/body/eval_jaxpr/bhqd,bhsd->bhqs/dot_general | solution.py:65
  100.1 2.9 %fusion.57 = f32[2,3,128,128]{3,2,1,0:T(8,128)S(1)} fusion(f32[3,512,2,128]{3,1,0,2:T(8,128)S(1)} %fusion.56, f32[2,3,512,128]{3,2,1,0:T(8,128)S(1)} %get-tuple-element.205, f32[2,3,128]{2,1,0:T(4,128)S(1)} %bitcast.139, f32[2,3,128]{2,1,0:T(4,128)S(1)} %max.4, f32[2,3,128,128]{3,2,1,0:T(8,128)S(1)} %get-tuple-element.223, ...), kind=kOutput, calls=%fused_computation.9.clone.1 | convolution fusion | flops 604962816 | bytes 3941376 | tf_op jit(solution)/shard_map/while/body/eval_jaxpr/bhqs,bhsd->bhqd/dot_general | solution.py:75
  105.0 1.6 %bitcast_reduce_fusion.2 = (f32[2,3,128]{2,1,0:T(4,128)S(1)}, f32[2,3,512,128]{3,2,1,0:T(8,128)S(1)}) fusion(f32[2,3,128,128]{3,2,1,0:T(8,128)S(1)} %get-tuple-element.240, f32[3,512,2,128]{3,1,0,2:T(8,128)S(1)} %fusion.54, f32[2,3,128]{2,1,0:T(4,128)S(1)} %bitcast.140, pred[512]{0:T(512)(128)(4,1)S(1)} %dynamic-slice_reduce_fusion.2), kind=kOutput, calls=%fused_computation.3.clone.1 | convolution fusion | flops 605551872 | bytes 3545600 | tf_op jit(solution)/shard_map/while/body/eval_jaxpr/bhqd,bhsd->bhqs/dot_general | solution.py:65
  107.8 2.9 %fusion.57 = f32[2,3,128,128]{3,2,1,0:T(8,128)S(1)} fusion(f32[3,512,2,128]{3,1,0,2:T(8,128)S(1)} %fusion.56, f32[2,3,512,128]{3,2,1,0:T(8,128)S(1)} %get-tuple-element.205, f32[2,3,128]{2,1,0:T(4,128)S(1)} %bitcast.139, f32[2,3,128]{2,1,0:T(4,128)S(1)} %max.4, f32[2,3,128,128]{3,2,1,0:T(8,128)S(1)} %get-tuple-element.223, ...), kind=kOutput, calls=%fused_computation.9.clone.1 | convolution fusion | flops 604962816 | bytes 3941376 | tf_op jit(solution)/shard_map/while/body/eval_jaxpr/bhqs,bhsd->bhqd/dot_general | solution.py:75
  111.0 2.2 %convolution_convert_fusion = bf16[256,3072]{1,0:T(8,128)(2,1)} fusion(bf16[384,3072]{1,0:T(8,128)(2,1)S(1)} %copy-done, bf16[48,8,2,128]{3,2,1,0:T(2,128)(2,1)S(1)} %bitcast.137), kind=kOutput, calls=%fused_computation.23 | convolution fusion | flops 604766208 | bytes 4128768 | tf_op jit(solution)/shard_map/dot_general | solution.py:101
  (77 shorter events, 20.3 us)
Async XLA Ops:
  7.2 103.9 %copy-start = (bf16[384,3072]{1,0:T(8,128)(2,1)S(1)}, bf16[384,3072]{1,0:T(8,128)(2,1)}, u32[]{:S(2)}) copy-start(bf16[384,3072]{1,0:T(8,128)(2,1)} %param.21) | copy-start | bytes 7077892
  7.2 66.0 %all-gather.2.cloned.1.call-start = ((), (), s32[]{:S(2)}) async-start(), calls=%async_computation | async-start | bytes 1671168 | tf_op jit(solution)/shard_map/all_gather | solution.py:80
  16.3 4.6 %copy-start.11 = (f32[2,2,3,128]{3,1,2,0:T(2,128)S(1)}, f32[2,2,3,128]{3,1,2,0:T(2,128)}, u32[]{:S(2)}) copy-start(f32[2,2,3,128]{3,1,2,0:T(2,128)} %param.19) | copy-start | bytes 18436
  21.7 3.3 %copy-start.9 = (f32[2,3,128]{0,2,1:T(8,128)S(1)}, f32[2,3,128]{0,2,1:T(8,128)}, u32[]{:S(2)}) copy-start(f32[2,3,128]{0,2,1:T(8,128)} %copy.48) | copy-start | bytes 9220
  21.7 3.8 %copy-start.7 = (f32[3,128,32]{1,2,0:T(8,128)S(1)}, f32[3,128,32]{1,2,0:T(8,128)}, u32[]{:S(2)}) copy-start(f32[3,128,32]{1,2,0:T(8,128)} %param.17) | copy-start | bytes 147460
  22.4 3.4 %copy-start.1 = (f32[2,128,1,3,128]{4,1,3,0,2:T(8,128)S(1)}, f32[2,128,1,3,128]{4,1,3,0,2:T(8,128)}, u32[]{:S(2)}) copy-start(f32[2,128,1,3,128]{4,1,3,0,2:T(8,128)} %copy.64) | copy-start | bytes 1179652
  22.4 3.4 %copy-start.5 = (f32[3,128,32]{1,2,0:T(8,128)S(1)}, f32[3,128,32]{1,2,0:T(8,128)}, u32[]{:S(2)}) copy-start(f32[3,128,32]{1,2,0:T(8,128)} %param.18) | copy-start | bytes 147460
  25.0 1.4 %copy-start.3 = (f32[2,128,3,128]{1,0,3,2:T(2,128)}, f32[2,128,3,128]{1,0,3,2:T(2,128)S(1)}, u32[]{:S(2)}) copy-start(f32[2,128,3,128]{1,0,3,2:T(2,128)S(1)} %get-tuple-element.115) | copy-start | bytes 1179652
  26.4 45.0 %copy-start.4 = (f32[2,128,3,128]{1,0,3,2:T(2,128)S(1)}, f32[2,128,3,128]{1,0,3,2:T(2,128)}, u32[]{:S(2)}) copy-start(f32[2,128,3,128]{1,0,3,2:T(2,128)} %copy-done.3) | copy-start | bytes 1179652
  26.4 45.9 %copy-start.2 = (f32[2,128,1,3,128]{4,1,3,0,2:T(8,128)S(1)}, f32[2,128,1,3,128]{4,1,3,0,2:T(8,128)}, u32[]{:S(2)}) copy-start(f32[2,128,1,3,128]{4,1,3,0,2:T(8,128)} %copy.64) | copy-start | bytes 1179652
  77.0 2.9 %copy-start.6 = (f32[3,128,32]{1,2,0:T(8,128)S(1)}, f32[3,128,32]{1,2,0:T(8,128)}, u32[]{:S(2)}) copy-start(f32[3,128,32]{1,2,0:T(8,128)} %param.18) | copy-start | bytes 147460
  77.0 2.9 %copy-start.8 = (f32[3,128,32]{1,2,0:T(8,128)S(1)}, f32[3,128,32]{1,2,0:T(8,128)}, u32[]{:S(2)}) copy-start(f32[3,128,32]{1,2,0:T(8,128)} %param.17) | copy-start | bytes 147460
  77.0 2.9 %copy-start.10 = (pred[4,512]{1,0:T(4,128)(4,1)S(1)}, pred[4,512]{1,0:T(4,128)(4,1)}, u32[]{:S(2)}) copy-start(pred[4,512]{1,0:T(4,128)(4,1)} %fusion.31) | copy-start | bytes 6148
Sparse Core Ops, SparseCore 0:
  27.2 41.7 all-gather.1
where the time goes:
time: 121 us; the launch traced here: 120 us
  blocking collectives  36.5 us (30%)
  matrix products  35.6 us (29%)
  local copies, waits for them, and re-layouts  22.8 us (19%)
  between operations  14.3 us (12%)
  other arithmetic  10.5 us (9%)
    psum x1, blocking collectives, per_device(): summed = lax.psum(local_sums, 'seq')  36.5 us
    dot_general x4, matrix products, absorb(): jnp.einsum('bhqs,bhsd->bhqd', weights, value_rebuilt, precision=highest)  11.5 us
    dot_general x4, matrix products, absorb(): jnp.einsum('bhqd,bhsd->bhqs', query_heads, key_rebuilt, precision=highest)  6.57 us
    dot_general x1, matrix products, per_device(): jnp.dot(flat_images, w_qkv, preferred_element_type=jnp.float32) + b_qkv  5.77 us
    squeeze x4, local copies, waits for them, and re-layouts, per_device(): result, unused = lax.scan(advance, start_state, stacked)  4.1 us
    another operation x1, local copies, waits for them, and re-layouts, per_device(): code_block.reshape(block_count, block_rows, sample_count - 0, 2, head_cou...  3.85 us
    dot_general x4, matrix products, absorb(): jnp.einsum('sbhr,hdr->bhsd', key_part, key_basis, precision=highest)  3.58 us
    dot_general x4, matrix products, absorb(): jnp.einsum('sbhr,hdr->bhsd', value_part, value_basis, precision=highest)  3.56 us
  transfers between devices with their start and end apart: 1, of which 0 were waited for; matrix products, arithmetic and copies ran while one was open for 8% of the time, Pallas kernels for 0%

commit v1 on v0

v1 whole, which is shorter than its diff:
```python
import functools
import math

import jax
import jax.numpy as jnp
from jax import lax
from jax.experimental import pallas as pl
from jax.experimental.pallas import tpu as pltpu
from jax.sharding import PartitionSpec as P

epsilon = 1e-06
highest = lax.Precision.HIGHEST
LANES = 128
ROW_CHUNKS = 6
MESH = pl.DeviceIdType.MESH
NT = (((1,), (1,)), ((), ()))


def natural_ring(mesh):
    try:
        names = list(mesh.axis_names)
        line = mesh.devices
        if names.index("seq") == 0:
            line = line.T
        chips = [d.coords for d in line[0][::2]]
        return all(
            sum(abs(a - b) for a, b in zip(one, two)) == 1 for one, two in zip(chips, chips[1:])
        )
    except Exception:
        return False


def attend_kernel(
    seq_count, natural,
    images, w_qkv, b_qkv, q_gain, k_gain, key_basis, value_basis, centers,
    attended, sums,
    x_s, w_s, b_s, qg_s, kg_s, kb_s, vb_s, cen_s,
    kv_acc, q_acc, kbd, vbd, kc_s, vc_s, qs_s, qbd,
    m_s, mn_s, ln_s, accn_s, acc_s,
    own, left_in, right_in, sib_own, sib_left, sib_right, part, part_in,
    in_sem, img_sem, small_sem,
    right_send, right_recv, left_send, left_recv,
    so_send, so_recv, sl_send, sl_recv, sr_send, sr_recv, p_send, p_recv,
):
    samples, tokens, width = x_s.shape
    heads, head_dim, rank = kb_s.shape
    codes = heads * rank
    side = heads * head_dim
    rows = samples * tokens
    chips = seq_count // 2
    half = chips // 2
    levels = seq_count.bit_length() - 1
    me = lax.axis_index("seq")
    core = me % 2
    chip = me // 2

    if natural:
        right_chip = (chip + 1) % chips
        left_chip = (chip + chips - 1) % chips
    else:
        def chip_at(pos):
            back = pos // half
            z = (1 - back) * pos + back * (chips - 1 - pos)
            return 2 * z + back

        far = chip % 2
        pos = (1 - far) * (chip // 2) + far * (chips - 1 - chip // 2)
        right_chip = chip_at((pos + 1) % chips)
        left_chip = chip_at((pos + chips - 1) % chips)
    right = right_chip * 2 + core
    left = left_chip * 2 + core
    sibling = chip * 2 + 1 - core
    partners = [me + bit * (1 - 2 * ((me // bit) % 2)) for bit in [1 << k for k in range(levels)]]

    barrier = pltpu.get_barrier_semaphore()
    greeted = [right, left] + partners
    for device in greeted:
        pl.semaphore_signal(barrier, inc=1, device_id={"seq": device}, device_id_type=MESH)

    step = width // ROW_CHUNKS
    img_copies, kv_copies = [], []
    for i in range(ROW_CHUNKS):
        cut = pl.ds(i * step, step)
        c = pltpu.make_async_copy(images.at[:, :, cut], x_s.at[:, :, cut], img_sem.at[i])
        c.start()
        img_copies.append(c)
        c = pltpu.make_async_copy(
            w_qkv.at[cut, pl.ds(side, 2 * side)], w_s.at[cut, pl.ds(side, 2 * side)], in_sem.at[i]
        )
        c.start()
        kv_copies.append(c)
    small = []
    pairs = [(b_qkv, b_s), (q_gain, qg_s), (k_gain, kg_s), (key_basis, kb_s), (value_basis, vb_s), (centers, cen_s)]
    for i, (src, dst) in enumerate(pairs):
        c = pltpu.make_async_copy(src, dst, small_sem.at[i])
        c.start()
        small.append(c)
    q_copy = pltpu.make_async_copy(
        w_qkv.at[:, pl.ds(0, side)], w_s.at[:, pl.ds(0, side)], in_sem.at[ROW_CHUNKS]
    )
    q_copy.start()

    for c in small:
        c.wait()
    kbd[...] = jnp.zeros_like(kbd)
    vbd[...] = jnp.zeros_like(vbd)
    for h in range(heads):
        kbd[h * head_dim:(h + 1) * head_dim, h * rank:(h + 1) * rank] = kb_s[h]
        vbd[h * head_dim:(h + 1) * head_dim, h * rank:(h + 1) * rank] = vb_s[h]

    for i in range(ROW_CHUNKS):
        img_copies[i].wait()
        kv_copies[i].wait()
        piece = jnp.dot(
            x_s[:, :, i * step:(i + 1) * step].reshape(rows, step),
            w_s[i * step:(i + 1) * step, side:3 * side],
            preferred_element_type=jnp.float32,
        )
        if i == 0:
            kv_acc[...] = piece
        else:
            kv_acc[...] += piece

    def gain_row(ref):
        return ref[...].reshape(1, head_dim)

    def bias_row(column):
        return b_s[pl.ds(column, head_dim)].reshape(1, head_dim)

    part[0] = jnp.zeros_like(part[0])
    for h in range(heads):
        cut = slice(h * head_dim, (h + 1) * head_dim)
        raw = kv_acc[:, cut] + bias_row(side + h * head_dim)
        mean_square = jnp.mean(raw * raw, axis=-1, keepdims=True)
        keys = raw * lax.rsqrt(mean_square + epsilon) * gain_row(kg_s)
        vcut = slice(side + h * head_dim, side + (h + 1) * head_dim)
        values = kv_acc[:, vcut] + bias_row(2 * side + h * head_dim)
        for b in range(samples):
            own_rows = slice(b * tokens, (b + 1) * tokens)
            for j, one in enumerate((keys, values)):
                line = (b * 2 + j) * heads + h
                part[0, line:line + 1, :] = jnp.sum(one[own_rows], axis=0, keepdims=True)
            kc_s[own_rows, cut] = keys[own_rows] - cen_s[b, 0, h:h + 1, :]
            vc_s[own_rows, cut] = values[own_rows] - cen_s[b, 1, h:h + 1, :]

    pl.semaphore_wait(barrier, len(greeted))
    started = []

    def send(src, dst, send_sem, recv_sem, device):
        c = pltpu.make_async_remote_copy(
            src_ref=src, dst_ref=dst, send_sem=send_sem, recv_sem=recv_sem,
            device_id={"seq": device}, device_id_type=MESH,
        )
        c.start()
        started.append(c)
        return c

    def goes(direction, distance, b):
        if distance < half or chips % 2:
            return True
        return (b < samples // 2) == (direction == 0)

    rights, lefts, sib_owns, sib_lefts, sib_rights = {}, {}, {}, {}, {}

    def send_right(distance, b):
        if distance <= half and goes(0, distance, b):
            src = own.at[b] if distance == 1 else left_in.at[distance - 2, b]
            rights[distance, b] = send(
                src, left_in.at[distance - 1, b], right_send.at[distance - 1, b],
                right_recv.at[distance - 1, b], right,
            )

    def send_left(distance, b):
        if distance <= half and goes(1, distance, b):
            src = own.at[b] if distance == 1 else right_in.at[distance - 2, b]
            lefts[distance, b] = send(
                src, right_in.at[distance - 1, b], left_send.at[distance - 1, b],
                left_recv.at[distance - 1, b], left,
            )

    for b in range(samples):
        own_rows = slice(b * tokens, (b + 1) * tokens)
        for j, (src, basis) in enumerate(((kc_s, kbd), (vc_s, vbd))):
            coded = jnp.dot(src[own_rows, :], basis[...], precision=highest, preferred_element_type=jnp.float32)
            own[b, j * codes:(j + 1) * codes, :] = coded.T[:codes].astype(jnp.bfloat16)
        send_right(1, b)
        send_left(1, b)
        sib_owns[b] = send(own.at[b], sib_own.at[b], so_send.at[b], so_recv.at[b], sibling)

    exchanges = []

    def exchange(level):
        if level > 0:
            exchanges[level - 1].wait_recv()
            part[level] = part[level - 1] + part_in[level - 1]
        if level < levels:
            exchanges.append(
                send(part.at[level], part_in.at[level], p_send.at[level], p_recv.at[level], partners[level])
            )

    exchange(0)

    q_copy.wait()
    q_acc[...] = jnp.dot(
        x_s[...].reshape(rows, width), w_s[:, :side], preferred_element_type=jnp.float32
    )
    scale = math.log2(math.e) / math.sqrt(head_dim)
    for h in range(heads):
        cut = slice(h * head_dim, (h + 1) * head_dim)
        raw = q_acc[:, cut] + bias_row(h * head_dim)
        mean_square = jnp.mean(raw * raw, axis=-1, keepdims=True)
        query = raw * lax.rsqrt(mean_square + epsilon) * gain_row(qg_s) * scale
        qs_s[:, cut] = query
        coded = jnp.dot(query, kbd[cut, :], precision=highest, preferred_element_type=jnp.float32)
        high = coded.astype(jnp.bfloat16)
        low = (coded - high.astype(jnp.float32)).astype(jnp.bfloat16)
        for b in range(samples):
            own_rows = slice(b * tokens, (b + 1) * tokens)
            qbd[b, h * tokens:(h + 1) * tokens, :LANES] = high[own_rows]
            qbd[b, h * tokens:(h + 1) * tokens, LANES:] = low[own_rows]

    def near(b):
        own_rows = slice(b * tokens, (b + 1) * tokens)
        for h in range(heads):
            cut = slice(h * head_dim, (h + 1) * head_dim)
            lines = slice(h * tokens, (h + 1) * tokens)
            scores = lax.dot_general(
                qs_s[own_rows, cut], kc_s[own_rows, cut], NT, precision=highest,
                preferred_element_type=jnp.float32,
            )
            top = jnp.max(scores, axis=-1, keepdims=True)
            weights = jnp.exp2(scores - top)
            total = jnp.sum(weights, axis=-1, keepdims=True)
            wide = jnp.broadcast_to(top, (tokens, LANES))
            m_s[b, lines, :] = wide
            mn_s[b, lines, :] = wide
            ln_s[b, lines, :] = jnp.broadcast_to(total, (tokens, LANES))
            accn_s[b, lines, :] = jnp.dot(
                weights, vc_s[own_rows, cut], precision=highest, preferred_element_type=jnp.float32
            )
        acc_s[b] = jnp.zeros_like(acc_s[b])

    def absorb(b, blocks):
        key_side = jnp.concatenate([r[:LANES, :] for r in blocks], axis=1)
        scores = jnp.dot(
            qbd[b], jnp.concatenate([key_side, key_side], axis=0), preferred_element_type=jnp.float32
        )
        before = m_s[b]
        now = jnp.maximum(before, jnp.max(scores, axis=-1, keepdims=True))
        weights = jnp.exp2(scores - now[:, :1]).astype(jnp.bfloat16)
        value_side = jnp.concatenate([r[codes:2 * codes, :] for r in blocks], axis=1)
        ones = jnp.ones((LANES - codes, value_side.shape[1]), jnp.bfloat16)
        added = lax.dot_general(
            weights, jnp.concatenate([value_side, ones], axis=0), NT, preferred_element_type=jnp.float32
        )
        acc_s[b] = acc_s[b] * jnp.exp2(before - now) + added
        m_s[b] = now

    for b in range(samples):
        near(b)

    waiting = {b: [] for b in range(samples)}
    for distance in range(1, half + 1):
        for b in range(samples):
            blocks = []
            if (distance, b) in rights:
                rights[distance, b].wait_recv()
                send_right(distance + 1, b)
                src = left_in.at[distance - 1, b]
                sib_lefts[distance, b] = send(
                    src, sib_left.at[distance - 1, b], sl_send.at[distance - 1, b],
                    sl_recv.at[distance - 1, b], sibling,
                )
                blocks.append(src)
            if (distance, b) in lefts:
                lefts[distance, b].wait_recv()
                send_left(distance + 1, b)
                src = right_in.at[distance - 1, b]
                sib_rights[distance, b] = send(
                    src, sib_right.at[distance - 1, b], sr_send.at[distance - 1, b],
                    sr_recv.at[distance - 1, b], sibling,
                )
                blocks.append(src)
            if distance == 1:
                sib_owns[b].wait_recv()
                blocks.append(sib_own.at[b])
            else:
                for copies, held in ((sib_lefts, sib_left), (sib_rights, sib_right)):
                    if (distance - 1, b) in copies:
                        copies[distance - 1, b].wait_recv()
                        blocks.append(held.at[distance - 2, b])
            absorb(b, blocks)
        if distance <= levels:
            exchange(distance)
    for level in range(half + 1, levels + 1):
        exchange(level)
    sums[...] = part[levels]

    for b in range(samples):
        own_rows = slice(b * tokens, (b + 1) * tokens)
        blocks = []
        for copies, held in ((sib_lefts, sib_left), (sib_rights, sib_right)):
            if (half, b) in copies:
                copies[half, b].wait_recv()
                blocks.append(held.at[half - 1, b])
        absorb(b, blocks)
        for h in range(heads):
            cut = slice(h * head_dim, (h + 1) * head_dim)
            lines = slice(h * tokens, (h + 1) * tokens)
            gathered = acc_s[b, lines, :]
            fade = jnp.exp2(mn_s[b, lines, :] - m_s[b, lines, :])
            total = gathered[:, codes:codes + 1] + (fade * ln_s[b, lines, :])[:, :1]
            rebuilt = lax.dot_general(
                gathered, vbd[cut, :], NT, precision=highest, preferred_element_type=jnp.float32
            )
            result = (rebuilt + fade * accn_s[b, lines, :]) / total + cen_s[b, 1, h:h + 1, :]
            attended[own_rows, cut] = result.astype(jnp.bfloat16)
    for c in started:
        c.wait_send()


def finish_kernel(length, refresh, attended, w_out, sums, centers, mixed, new_centers):
    samples, pair, heads, head_dim = new_centers.shape
    tokens = attended.shape[0] // samples
    product = jnp.dot(attended[...], w_out[...], preferred_element_type=jnp.float32)
    mixed[...] = product.astype(jnp.bfloat16).reshape(mixed.shape)

    @pl.when(pl.program_id(0) == 0)
    def _():
        for b in range(samples):
            for j in range(pair):
                for h in range(heads):
                    line = (b * pair + j) * heads + h
                    fresh = sums[line:line + 1, :] / length
                    old = centers[b, j, h:h + 1, :]
                    new_centers[b, j, h:h + 1, :] = jnp.where(refresh[j, h] == 1, fresh, old)


def per_device(
    seq_count, natural,
    images, w_qkv, b_qkv, q_gain, k_gain, key_basis, value_basis, centers, refresh, w_out
):
    samples, tokens, width = images.shape
    heads, head_dim, rank = key_basis.shape
    side = heads * head_dim
    rows = samples * tokens
    codes = heads * rank
    chips = seq_count // 2
    half = chips // 2
    levels = seq_count.bit_length() - 1
    lines = -(-samples * 2 * heads // 8) * 8
    f32, bf16 = jnp.float32, jnp.bfloat16
    any_spec = pl.BlockSpec(memory_space=pl.ANY)
    vmem_spec = pl.BlockSpec(memory_space=pltpu.VMEM)
    dma = pltpu.SemaphoreType.DMA
    block = (samples, 2 * codes, tokens)
    stat = pltpu.VMEM((samples, heads * tokens, LANES), f32)
    attended, sums = pl.pallas_call(
        functools.partial(attend_kernel, seq_count, natural),
        out_shape=(
            jax.ShapeDtypeStruct((rows, side), bf16),
            jax.ShapeDtypeStruct((lines, head_dim), f32),
        ),
        in_specs=[any_spec] * 8,
        out_specs=(vmem_spec, vmem_spec),
        scratch_shapes=[
            pltpu.VMEM(images.shape, bf16),
            pltpu.VMEM(w_qkv.shape, bf16),
            pltpu.VMEM(b_qkv.shape, f32),
            pltpu.VMEM(q_gain.shape, f32),
            pltpu.VMEM(k_gain.shape, f32),
            pltpu.VMEM(key_basis.shape, f32),
            pltpu.VMEM(value_basis.shape, f32),
            pltpu.VMEM(centers.shape, f32),
            pltpu.VMEM((rows, 2 * side), f32),
            pltpu.VMEM((rows, side), f32),
            pltpu.VMEM((side, LANES), f32),
            pltpu.VMEM((side, LANES), f32),
            pltpu.VMEM((rows, side), f32),
            pltpu.VMEM((rows, side), f32),
            pltpu.VMEM((rows, side), f32),
            pltpu.VMEM((samples, heads * tokens, 2 * LANES), bf16),
            stat, stat, stat, stat, stat,
            pltpu.VMEM(block, bf16),
            pltpu.VMEM((half,) + block, bf16),
            pltpu.VMEM((half,) + block, bf16),
            pltpu.VMEM(block, bf16),
            pltpu.VMEM((half,) + block, bf16),
            pltpu.VMEM((half,) + block, bf16),
            pltpu.VMEM((levels + 1, lines, head_dim), f32),
            pltpu.VMEM((levels, lines, head_dim), f32),
            dma((ROW_CHUNKS + 1,)), dma((ROW_CHUNKS,)), dma((6,)),
            dma((half, samples)), dma((half, samples)), dma((half, samples)), dma((half, samples)),
            dma((samples,)), dma((samples,)),
            dma((half, samples)), dma((half, samples)), dma((half, samples)), dma((half, samples)),
            dma((levels,)), dma((levels,)),
        ],
        compiler_params=pltpu.CompilerParams(
            collective_id=0, has_side_effects=True, vmem_limit_bytes=40 << 20
        ),
        name="attend",
    )(images, w_qkv, b_qkv, q_gain, k_gain, key_basis, value_basis, centers)

    tile = width // 3
    mixed, new_centers = pl.pallas_call(
        functools.partial(finish_kernel, float(tokens * seq_count)),
        grid=(width // tile,),
        out_shape=(
            jax.ShapeDtypeStruct(images.shape, bf16),
            jax.ShapeDtypeStruct(centers.shape, f32),
        ),
        in_specs=[
            pl.BlockSpec(memory_space=pltpu.SMEM),
            pl.BlockSpec((rows, side), lambda n: (0, 0)),
            pl.BlockSpec((side, tile), lambda n: (0, n)),
            pl.BlockSpec((lines, head_dim), lambda n: (0, 0)),
            pl.BlockSpec(centers.shape, lambda n: (0, 0, 0, 0)),
        ],
        out_specs=(
            pl.BlockSpec((samples, tokens, tile), lambda n: (0, 0, n)),
            pl.BlockSpec(centers.shape, lambda n: (0, 0, 0, 0)),
        ),
        compiler_params=pltpu.CompilerParams(vmem_limit_bytes=16 << 20),
        name="finish",
    )(refresh, attended, w_out, sums, centers)
    return mixed, new_centers


def solution(mesh):
    return jax.shard_map(
        functools.partial(per_device, mesh.shape["seq"], natural_ring(mesh)),
        mesh=mesh,
        in_specs=(
            P("groups", "seq", None),
            P(),
            P(),
            P(),
            P(),
            P(),
            P(),
            P("groups", None, None, None),
            P(),
            P(),
        ),
        out_specs=(P("groups", "seq", None), P("groups", None, None, None)),
        check_vma=False,
    )
```

time: 121 us -> 41.3 us (0.34)
  blocking collectives: 36.5 us -> 0 us
  matrix products: 35.6 us -> 0 us
  Pallas kernels: 0 us -> 30.7 us
  between operations: 14.3 us -> 0.67 us
  local copies, waits for them, and re-layouts: 22.8 us -> 9.58 us
  other arithmetic: 10.5 us -> 0 us
    psum x1 -> x0, blocking collectives: 36.5 us -> none  [per_device(): summed = lax.psum(local_sums, 'seq')]
    dot_general x22 -> x0, matrix products: 35.6 us -> none  [the longest x4 11.5 us: absorb(): jnp.einsum('bhqs,bhsd->bhqd', weights, value_rebuilt, precision=highest)]
    pallas_call x0 -> x2, Pallas kernels: none -> 30.7 us  [the longest x1 27.6 us: per_device(): pl.pallas_call(functools.partial(attend_kernel, seq_count, natural), out_...]
    unnamed x27 -> x17, local copies, waits for them, and re-layouts: 2.56 us -> 8.98 us
    reduce_sum x8 -> x0, other arithmetic: 6.22 us -> none  [the longest x1 2.55 us: per_device(): jnp.sum(keys_local, axis=1)]
    squeeze x4 -> x0, local copies, waits for them, and re-layouts: 4.1 us -> none  [per_device(): result, unused = lax.scan(advance, start_state, stacked)]
    another operation x1 -> x0, local copies, waits for them, and re-layouts: 3.85 us -> none  [per_device(): code_block.reshape(block_count, block_rows, sample_count - 0, 2, head_cou...]
    reduce_sum x2 -> x0, local copies, waits for them, and re-layouts: 3.22 us -> none  [the longest x1 1.61 us: per_device(): jnp.sum(keys_local, axis=1)]
  transfers between devices with their start and end apart: 1 -> 0, of which waited for: 0 -> 0; matrix products, arithmetic and copies ran while one was open for 8% -> 0% of each run, Pallas kernels for 0% -> 0%
where the time goes in v1:
time: 41.3 us; the launch traced here: 41 us
  Pallas kernels  30.7 us (74%)
  local copies, waits for them, and re-layouts  9.58 us (23%)
  between operations  0.67 us (2%)
    pallas_call x1, Pallas kernels, per_device(): pl.pallas_call(functools.partial(attend_kernel, seq_count, natural), out_...  27.6 us
    unnamed x17, local copies, waits for them, and re-layouts  8.98 us
    pallas_call x1, Pallas kernels, per_device(): pl.pallas_call(functools.partial(finish_kernel, float(tokens * seq_count)...  3.12 us

profile of v1, /device:TPU:0, one launch (start us, length us, event | category | flops | bytes accessed | tf_op | source)
XLA Modules:
  0.0 41.0 jit_solution(8250541486035629513)
XLA Ops:
  0.6 0.7 %copy.14.centers = f32[2,2,3,128]{3,2,1,0:T(4,128)S(1)} copy(f32[2,2,3,128]{3,1,2,0:T(2,128)} %param.17) | data formatting | bytes 12288 | tf_op args[7]
  1.3 0.9 %copy.12.key_basis = f32[3,128,32]{2,1,0:T(8,128)S(1)} copy(f32[3,128,32]{1,2,0:T(8,128)} %param.15) | data formatting | bytes 98304 | tf_op args[5]
  2.3 0.9 %copy.13.value_basis = f32[3,128,32]{2,1,0:T(8,128)S(1)} copy(f32[3,128,32]{1,2,0:T(8,128)} %param.16) | data formatting | bytes 98304 | tf_op args[6]
  3.2 0.0 copy-start
  3.2 3.0 %copy-done = bf16[3072,1152]{1,0:T(8,128)(2,1)S(1)} copy-done((bf16[3072,1152]{1,0:T(8,128)(2,1)S(1)}, bf16[3072,1152]{1,0:T(8,128)(2,1)}, u32[]{:S(2)}) %copy-start) | copy-done | bytes 7077912
  6.2 0.0 copy-start.2
  6.2 1.4 %copy-done.2 = bf16[2,128,3072]{2,1,0:T(8,128)(2,1)S(1)} copy-done((bf16[2,128,3072]{2,1,0:T(8,128)(2,1)S(1)}, bf16[2,128,3072]{2,1,0:T(8,128)(2,1)}, u32[]{:S(2)}) %copy-start.2) | copy-done | bytes 1572888
  7.6 0.0 copy-start.3
  7.6 0.7 %copy-done.3 = f32[1152]{0:T(1024)S(1)} copy-done((f32[1152]{0:T(1024)S(1)}, f32[1152]{0:T(1024)}, u32[]{:S(2)}) %copy-start.3) | copy-done | bytes 4632
  8.3 0.0 copy-start.5
  8.3 0.7 %copy-done.5 = f32[128]{0:T(128)S(1)} copy-done((f32[128]{0:T(128)S(1)}, f32[128]{0:T(128)}, u32[]{:S(2)}) %copy-start.5) | copy-done | bytes 536
  9.0 0.0 copy-start.6
  9.0 0.7 %copy-done.6 = f32[128]{0:T(128)S(1)} copy-done((f32[128]{0:T(128)S(1)}, f32[128]{0:T(128)}, u32[]{:S(2)}) %copy-start.6) | copy-done | bytes 536
  9.6 0.0 copy-start.1
  9.6 0.0 copy-start.4
  9.6 27.6 %attend.1 = (bf16[256,384]{1,0:T(8,128)(2,1)S(1)}, f32[16,128]{1,0:T(8,128)S(1)}) custom-call(bf16[2,128,3072]{2,1,0:T(8,128)(2,1)S(1)} %copy-done.2, bf16[3072,1152]{1,0:T(8,128)(2,1)S(1)} %copy-done, f32[1152]{0:T(1024)S(1)} %copy-done.3, f32[128]{0:T(128)S(1)} %copy-done.5, f32[128]{0:T(128)S(1)} %copy-done.6, f32[3,128,32]{2,1,0:T(8,128)S(1)} %copy.12.key_basis, ...), custom_call_target="tpu_custom_call" | custom-call | tf_op jit(solution)/shard_map/attend/pallas_call | solution.py:358
  37.2 0.0 copy-done.1
  37.2 0.0 copy-done.4
  37.2 3.1 %finish.1 = (bf16[2,128,3072]{2,1,0:T(8,128)(2,1)}, f32[2,2,3,128]{3,2,1,0:T(4,128)S(1)}) custom-call(s32[2,3]{1,0:T(2,128)S(1)} %copy-done.4, bf16[256,384]{1,0:T(8,128)(2,1)S(1)} %get-tuple-element.4.attended, bf16[384,3072]{1,0:T(8,128)(2,1)S(1)} %copy-done.1, f32[16,128]{1,0:T(8,128)S(1)} %get-tuple-element.5.sums, f32[2,2,3,128]{3,2,1,0:T(4,128)S(1)} %copy.14.centers), custom_call_target="tpu_custom_call" | custom-call | tf_op jit(solution)/shard_map/finish/pallas_call | solution.py:405
  40.4 0.6 %copy.16 = f32[2,2,3,128]{3,1,2,0:T(2,128)} copy(f32[2,2,3,128]{3,2,1,0:T(4,128)S(1)} %get-tuple-element.7) | data formatting | bytes 12288 | tf_op jit(solution)/shard_map/finish/pallas_call | solution.py:405
Async XLA Ops:
  3.2 3.0 %copy-start = (bf16[3072,1152]{1,0:T(8,128)(2,1)S(1)}, bf16[3072,1152]{1,0:T(8,128)(2,1)}, u32[]{:S(2)}) copy-start(bf16[3072,1152]{1,0:T(8,128)(2,1)} %w_qkv.1) | copy-start | bytes 21233668
  6.2 1.4 %copy-start.2 = (bf16[2,128,3072]{2,1,0:T(8,128)(2,1)S(1)}, bf16[2,128,3072]{2,1,0:T(8,128)(2,1)}, u32[]{:S(2)}) copy-start(bf16[2,128,3072]{2,1,0:T(8,128)(2,1)} %images.1) | copy-start | bytes 4718596
  7.6 0.7 %copy-start.3 = (f32[1152]{0:T(1024)S(1)}, f32[1152]{0:T(1024)}, u32[]{:S(2)}) copy-start(f32[1152]{0:T(1024)} %b_qkv.1) | copy-start | bytes 13828
  8.3 0.7 %copy-start.5 = (f32[128]{0:T(128)S(1)}, f32[128]{0:T(128)}, u32[]{:S(2)}) copy-start(f32[128]{0:T(128)} %q_gain.1) | copy-start | bytes 1540
  9.0 0.7 %copy-start.6 = (f32[128]{0:T(128)S(1)}, f32[128]{0:T(128)}, u32[]{:S(2)}) copy-start(f32[128]{0:T(128)} %k_gain.1) | copy-start | bytes 1540
  9.6 27.6 %copy-start.1 = (bf16[384,3072]{1,0:T(8,128)(2,1)S(1)}, bf16[384,3072]{1,0:T(8,128)(2,1)}, u32[]{:S(2)}) copy-start(bf16[384,3072]{1,0:T(8,128)(2,1)} %w_out.1) | copy-start | bytes 7077892
  9.6 27.6 %copy-start.4 = (s32[2,3]{1,0:T(2,128)S(1)}, s32[2,3]{1,0:T(2,128)}, u32[]{:S(2)}) copy-start(s32[2,3]{1,0:T(2,128)} %refresh.1) | copy-start | bytes 76

commit v2 on v1

--- a/solution.py
+++ b/solution.py
@@ -12,6 +12,7 @@
 highest = lax.Precision.HIGHEST
 LANES = 128
 ROW_CHUNKS = 6
+OUT_TILES = 6
 MESH = pl.DeviceIdType.MESH
 NT = (((1,), (1,)), ((), ()))
 
@@ -43,7 +44,7 @@
     so_send, so_recv, sl_send, sl_recv, sr_send, sr_recv, p_send, p_recv,
 ):
     samples, tokens, width = x_s.shape
-    heads, head_dim, rank = kb_s.shape
+    heads, rank, head_dim = kb_s.shape
     codes = heads * rank
     side = heads * head_dim
     rows = samples * tokens
@@ -105,8 +106,8 @@
     kbd[...] = jnp.zeros_like(kbd)
     vbd[...] = jnp.zeros_like(vbd)
     for h in range(heads):
-        kbd[h * head_dim:(h + 1) * head_dim, h * rank:(h + 1) * rank] = kb_s[h]
-        vbd[h * head_dim:(h + 1) * head_dim, h * rank:(h + 1) * rank] = vb_s[h]
+        kbd[h * rank:(h + 1) * rank, h * head_dim:(h + 1) * head_dim] = kb_s[h]
+        vbd[h * rank:(h + 1) * rank, h * head_dim:(h + 1) * head_dim] = vb_s[h]
 
     for i in range(ROW_CHUNKS):
         img_copies[i].wait()
@@ -140,8 +141,8 @@
             for j, one in enumerate((keys, values)):
                 line = (b * 2 + j) * heads + h
                 part[0, line:line + 1, :] = jnp.sum(one[own_rows], axis=0, keepdims=True)
-            kc_s[own_rows, cut] = keys[own_rows] - cen_s[b, 0, h:h + 1, :]
-            vc_s[own_rows, cut] = values[own_rows] - cen_s[b, 1, h:h + 1, :]
+            kc_s[own_rows, cut] = keys[own_rows] - cen_s[b, h, 0:1, :]
+            vc_s[own_rows, cut] = values[own_rows] - cen_s[b, h, 1:2, :]
 
     pl.semaphore_wait(barrier, len(greeted))
     started = []
@@ -181,8 +182,11 @@
     for b in range(samples):
         own_rows = slice(b * tokens, (b + 1) * tokens)
         for j, (src, basis) in enumerate(((kc_s, kbd), (vc_s, vbd))):
-            coded = jnp.dot(src[own_rows, :], basis[...], precision=highest, preferred_element_type=jnp.float32)
-            own[b, j * codes:(j + 1) * codes, :] = coded.T[:codes].astype(jnp.bfloat16)
+            coded = lax.dot_general(
+                basis[:codes, :], src[own_rows, :], NT, precision=highest,
+                preferred_element_type=jnp.float32,
+            )
+            own[b, j * codes:(j + 1) * codes, :] = coded.astype(jnp.bfloat16)
         send_right(1, b)
         send_left(1, b)
         sib_owns[b] = send(own.at[b], sib_own.at[b], so_send.at[b], so_recv.at[b], sibling)
@@ -211,7 +215,9 @@
         mean_square = jnp.mean(raw * raw, axis=-1, keepdims=True)
         query = raw * lax.rsqrt(mean_square + epsilon) * gain_row(qg_s) * scale
         qs_s[:, cut] = query
-        coded = jnp.dot(query, kbd[cut, :], precision=highest, preferred_element_type=jnp.float32)
+        coded = lax.dot_general(
+            query, kbd[:, cut], NT, precision=highest, preferred_element_type=jnp.float32
+        )
         high = coded.astype(jnp.bfloat16)
         low = (coded - high.astype(jnp.float32)).astype(jnp.bfloat16)
         for b in range(samples):
@@ -310,30 +316,35 @@
             gathered = acc_s[b, lines, :]
             fade = jnp.exp2(mn_s[b, lines, :] - m_s[b, lines, :])
             total = gathered[:, codes:codes + 1] + (fade * ln_s[b, lines, :])[:, :1]
-            rebuilt = lax.dot_general(
-                gathered, vbd[cut, :], NT, precision=highest, preferred_element_type=jnp.float32
-            )
-            result = (rebuilt + fade * accn_s[b, lines, :]) / total + cen_s[b, 1, h:h + 1, :]
+            rebuilt = jnp.dot(
+                gathered, vbd[:, cut], precision=highest, preferred_element_type=jnp.float32
+            )
+            result = (rebuilt + fade * accn_s[b, lines, :]) / total + cen_s[b, h, 1:2, :]
             attended[own_rows, cut] = result.astype(jnp.bfloat16)
     for c in started:
         c.wait_send()
 
 
-def finish_kernel(length, refresh, attended, w_out, sums, centers, mixed, new_centers):
-    samples, pair, heads, head_dim = new_centers.shape
-    tokens = attended.shape[0] // samples
-    product = jnp.dot(attended[...], w_out[...], preferred_element_type=jnp.float32)
-    mixed[...] = product.astype(jnp.bfloat16).reshape(mixed.shape)
-
-    @pl.when(pl.program_id(0) == 0)
-    def _():
-        for b in range(samples):
-            for j in range(pair):
-                for h in range(heads):
-                    line = (b * pair + j) * heads + h
-                    fresh = sums[line:line + 1, :] / length
-                    old = centers[b, j, h:h + 1, :]
-                    new_centers[b, j, h:h + 1, :] = jnp.where(refresh[j, h] == 1, fresh, old)
+def finish_kernel(length, refresh, attended, w_out, sums, centers, mixed, new_centers, tiles, sem):
+    samples, heads, pair, head_dim = new_centers.shape
+    count, _, _, tile = tiles.shape
+    copies = []
+    for n in range(count):
+        cut = slice(n * tile, (n + 1) * tile)
+        product = jnp.dot(attended[...], w_out[:, cut], preferred_element_type=jnp.float32)
+        tiles[n] = product.astype(jnp.bfloat16).reshape(tiles.shape[1:])
+        c = pltpu.make_async_copy(tiles.at[n], mixed.at[:, :, pl.ds(n * tile, tile)], sem.at[n])
+        c.start()
+        copies.append(c)
+    for b in range(samples):
+        for j in range(pair):
+            for h in range(heads):
+                line = (b * pair + j) * heads + h
+                fresh = sums[line:line + 1, :] / length
+                old = centers[b, h, j:j + 1, :]
+                new_centers[b, h, j:j + 1, :] = jnp.where(refresh[j, h] == 1, fresh, old)
+    for c in copies:
+        c.wait()
 
 
 def per_device(
@@ -342,6 +353,9 @@
 ):
     samples, tokens, width = images.shape
     heads, head_dim, rank = key_basis.shape
+    key_basis = jnp.swapaxes(key_basis, 1, 2)
+    value_basis = jnp.swapaxes(value_basis, 1, 2)
+    centers = jnp.transpose(centers, (0, 2, 1, 3))
     side = heads * head_dim
     rows = samples * tokens
     codes = heads * rank
@@ -350,7 +364,7 @@
     levels = seq_count.bit_length() - 1
     lines = -(-samples * 2 * heads // 8) * 8
     f32, bf16 = jnp.float32, jnp.bfloat16
-    any_spec = pl.BlockSpec(memory_space=pl.ANY)
+    hbm_spec = pl.BlockSpec(memory_space=pltpu.HBM)
     vmem_spec = pl.BlockSpec(memory_space=pltpu.VMEM)
     dma = pltpu.SemaphoreType.DMA
     block = (samples, 2 * codes, tokens)
@@ -361,7 +375,7 @@
             jax.ShapeDtypeStruct((rows, side), bf16),
             jax.ShapeDtypeStruct((lines, head_dim), f32),
         ),
-        in_specs=[any_spec] * 8,
+        in_specs=[hbm_spec] * 8,
         out_specs=(vmem_spec, vmem_spec),
         scratch_shapes=[
             pltpu.VMEM(images.shape, bf16),
@@ -374,8 +388,8 @@
             pltpu.VMEM(centers.shape, f32),
             pltpu.VMEM((rows, 2 * side), f32),
             pltpu.VMEM((rows, side), f32),
-            pltpu.VMEM((side, LANES), f32),
-            pltpu.VMEM((side, LANES), f32),
+            pltpu.VMEM((LANES, side), f32),
+            pltpu.VMEM((LANES, side), f32),
             pltpu.VMEM((rows, side), f32),
             pltpu.VMEM((rows, side), f32),
             pltpu.VMEM((rows, side), f32),
@@ -399,31 +413,28 @@
             collective_id=0, has_side_effects=True, vmem_limit_bytes=40 << 20
         ),
         name="attend",
-    )(images, w_qkv, b_qkv, q_gain, k_gain, key_basis, value_basis, centers)
-
-    tile = width // 3
+    )(*[
+        pltpu.with_memory_space_constraint(a, pltpu.HBM)
+        for a in (images, w_qkv, b_qkv, q_gain, k_gain, key_basis, value_basis, centers)
+    ])
+
+    tile = width // OUT_TILES
     mixed, new_centers = pl.pallas_call(
         functools.partial(finish_kernel, float(tokens * seq_count)),
-        grid=(width // tile,),
         out_shape=(
             jax.ShapeDtypeStruct(images.shape, bf16),
             jax.ShapeDtypeStruct(centers.shape, f32),
         ),
-        in_specs=[
-            pl.BlockSpec(memory_space=pltpu.SMEM),
-            pl.BlockSpec((rows, side), lambda n: (0, 0)),
-            pl.BlockSpec((side, tile), lambda n: (0, n)),
-            pl.BlockSpec((lines, head_dim), lambda n: (0, 0)),
-            pl.BlockSpec(centers.shape, lambda n: (0, 0, 0, 0)),
+        in_specs=[pl.BlockSpec(memory_space=pltpu.SMEM)] + [vmem_spec] * 4,
+        out_specs=(hbm_spec, vmem_spec),
+        scratch_shapes=[
+            pltpu.VMEM((OUT_TILES, samples, tokens, tile), bf16),
+            dma((OUT_TILES,)),
         ],
-        out_specs=(
-            pl.BlockSpec((samples, tokens, tile), lambda n: (0, 0, n)),
-            pl.BlockSpec(centers.shape, lambda n: (0, 0, 0, 0)),
-        ),
         compiler_params=pltpu.CompilerParams(vmem_limit_bytes=16 << 20),
         name="finish",
     )(refresh, attended, w_out, sums, centers)
-    return mixed, new_centers
+    return mixed, jnp.transpose(new_centers, (0, 2, 1, 3))
 
 
 def solution(mesh):

time: 41.3 us -> 32.5 us (0.79)
  local copies, waits for them, and re-layouts: 9.58 us -> 0.01 us
  Pallas kernels: 30.7 us -> 31.6 us
    unnamed x17 -> x6, local copies, waits for them, and re-layouts: 8.98 us -> 0.01 us
    pallas_call x1, Pallas kernels: 27.6 us -> 28.7 us  [per_device(): pl.pallas_call(functools.partial(attend_kernel, seq_count, natural), out_...]
    pallas_call x1 -> x0, local copies, waits for them, and re-layouts: 0.6 us -> none  [per_device(): pl.pallas_call(functools.partial(finish_kernel, float(tokens * seq_count)...]
where the time goes in v2:
time: 32.5 us; the launch traced here: 32.3 us
  Pallas kernels  31.6 us (97%)
  between operations  0.69 us (2%)
    pallas_call x1, Pallas kernels, per_device(): pl.pallas_call(functools.partial(attend_kernel, seq_count, natural), out_...  28.7 us
    pallas_call x1, Pallas kernels, per_device(): pl.pallas_call(functools.partial(finish_kernel, float(tokens * seq_count)...  2.89 us

profile of v2, /device:TPU:0, one launch (start us, length us, event | category | flops | bytes accessed | tf_op | source)
XLA Modules:
  0.0 32.3 jit_solution(7838661918292156374)
XLA Ops:
  0.6 0.0 copy-start
  0.6 0.0 copy-start.1
  0.7 0.0 copy-start.2
  0.7 28.7 %attend.1 = (bf16[256,384]{1,0:T(8,128)(2,1)S(1)}, f32[16,128]{1,0:T(8,128)S(1)}) custom-call(bf16[2,128,3072]{2,1,0:T(8,128)(2,1)} %images.1, bf16[3072,1152]{1,0:T(8,128)(2,1)} %w_qkv.1, f32[1152]{0:T(1024)} %b_qkv.1, f32[128]{0:T(128)} %q_gain.1, f32[128]{0:T(128)} %k_gain.1, f32[3,32,128]{2,1,0:T(8,128)} %bitcast.6, f32[3,32,128]{2,1,0:T(8,128)} %bitcast.7, ...), custom_call_target="tpu_custom_call" | custom-call | tf_op jit(solution)/shard_map/attend/pallas_call | solution.py:372
  29.4 0.0 copy-done
  29.4 0.0 copy-done.1
  29.4 0.0 copy-done.2
  29.4 2.9 %finish.1 = (bf16[2,128,3072]{2,1,0:T(8,128)(2,1)}, f32[2,3,2,128]{3,2,1,0:T(2,128)}) custom-call(s32[2,3]{1,0:T(2,128)S(1)} %copy-done.2, bf16[256,384]{1,0:T(8,128)(2,1)S(1)} %get-tuple-element.6.attended, bf16[384,3072]{1,0:T(8,128)(2,1)S(1)} %copy-done, f32[16,128]{1,0:T(8,128)S(1)} %get-tuple-element.7.sums, f32[2,3,2,128]{3,2,1,0:T(2,128)S(1)} %bitcast.5), custom_call_target="tpu_custom_call" | custom-call | tf_op jit(solution)/shard_map/finish/pallas_call | solution.py:422
Async XLA Ops:
  0.6 28.8 %copy-start = (bf16[384,3072]{1,0:T(8,128)(2,1)S(1)}, bf16[384,3072]{1,0:T(8,128)(2,1)}, u32[]{:S(2)}) copy-start(bf16[384,3072]{1,0:T(8,128)(2,1)} %w_out.1) | copy-start | bytes 7077892
  0.6 28.8 %copy-start.1 = (f32[2,2,3,128]{3,1,2,0:T(2,128)S(1)}, f32[2,2,3,128]{3,1,2,0:T(2,128)}, u32[]{:S(2)}) copy-start(f32[2,2,3,128]{3,1,2,0:T(2,128)} %param.17) | copy-start | bytes 18436
  0.7 28.8 %copy-start.2 = (s32[2,3]{1,0:T(2,128)S(1)}, s32[2,3]{1,0:T(2,128)}, u32[]{:S(2)}) copy-start(s32[2,3]{1,0:T(2,128)} %refresh.1) | copy-start | bytes 76

commit v3 on v2

--- a/solution.py
+++ b/solution.py
@@ -9,7 +9,7 @@
 from jax.sharding import PartitionSpec as P
 
 epsilon = 1e-06
-highest = lax.Precision.HIGHEST
+highest = lax.Precision.HIGH
 LANES = 128
 ROW_CHUNKS = 6
 OUT_TILES = 6
@@ -78,6 +78,12 @@
     for device in greeted:
         pl.semaphore_signal(barrier, inc=1, device_id={"seq": device}, device_id_type=MESH)
 
+    small = []
+    pairs = [(b_qkv, b_s), (q_gain, qg_s), (k_gain, kg_s), (key_basis, kb_s), (value_basis, vb_s), (centers, cen_s)]
+    for i, (src, dst) in enumerate(pairs):
+        c = pltpu.make_async_copy(src, dst, small_sem.at[i])
+        c.start()
+        small.append(c)
     step = width // ROW_CHUNKS
     img_copies, kv_copies = [], []
     for i in range(ROW_CHUNKS):
@@ -90,12 +96,6 @@
         )
         c.start()
         kv_copies.append(c)
-    small = []
-    pairs = [(b_qkv, b_s), (q_gain, qg_s), (k_gain, kg_s), (key_basis, kb_s), (value_basis, vb_s), (centers, cen_s)]
-    for i, (src, dst) in enumerate(pairs):
-        c = pltpu.make_async_copy(src, dst, small_sem.at[i])
-        c.start()
-        small.append(c)
     q_copy = pltpu.make_async_copy(
         w_qkv.at[:, pl.ds(0, side)], w_s.at[:, pl.ds(0, side)], in_sem.at[ROW_CHUNKS]
     )
@@ -179,18 +179,6 @@
                 left_recv.at[distance - 1, b], left,
             )
 
-    for b in range(samples):
-        own_rows = slice(b * tokens, (b + 1) * tokens)
-        for j, (src, basis) in enumerate(((kc_s, kbd), (vc_s, vbd))):
-            coded = lax.dot_general(
-                basis[:codes, :], src[own_rows, :], NT, precision=highest,
-                preferred_element_type=jnp.float32,
-            )
-            own[b, j * codes:(j + 1) * codes, :] = coded.astype(jnp.bfloat16)
-        send_right(1, b)
-        send_left(1, b)
-        sib_owns[b] = send(own.at[b], sib_own.at[b], so_send.at[b], so_recv.at[b], sibling)
-
     exchanges = []
 
     def exchange(level):
@@ -203,6 +191,18 @@
             )
 
     exchange(0)
+
+    for b in range(samples):
+        own_rows = slice(b * tokens, (b + 1) * tokens)
+        for j, (src, basis) in enumerate(((kc_s, kbd), (vc_s, vbd))):
+            coded = lax.dot_general(
+                basis[:codes, :], src[own_rows, :], NT, precision=highest,
+                preferred_element_type=jnp.float32,
+            )
+            own[b, j * codes:(j + 1) * codes, :] = coded.astype(jnp.bfloat16)
+        send_right(1, b)
+        send_left(1, b)
+        sib_owns[b] = send(own.at[b], sib_own.at[b], so_send.at[b], so_recv.at[b], sibling)
 
     q_copy.wait()
     q_acc[...] = jnp.dot(
@@ -262,31 +262,30 @@
         acc_s[b] = acc_s[b] * jnp.exp2(before - now) + added
         m_s[b] = now
 
-    for b in range(samples):
-        near(b)
-
-    waiting = {b: [] for b in range(samples)}
-    for distance in range(1, half + 1):
+    def pass_on(distance):
+        for b in range(samples):
+            if (distance, b) in rights:
+                rights[distance, b].wait_recv()
+                send_right(distance + 1, b)
+                sib_lefts[distance, b] = send(
+                    left_in.at[distance - 1, b], sib_left.at[distance - 1, b],
+                    sl_send.at[distance - 1, b], sl_recv.at[distance - 1, b], sibling,
+                )
+            if (distance, b) in lefts:
+                lefts[distance, b].wait_recv()
+                send_left(distance + 1, b)
+                sib_rights[distance, b] = send(
+                    right_in.at[distance - 1, b], sib_right.at[distance - 1, b],
+                    sr_send.at[distance - 1, b], sr_recv.at[distance - 1, b], sibling,
+                )
+
+    def absorb_stage(distance):
         for b in range(samples):
             blocks = []
             if (distance, b) in rights:
-                rights[distance, b].wait_recv()
-                send_right(distance + 1, b)
-                src = left_in.at[distance - 1, b]
-                sib_lefts[distance, b] = send(
-                    src, sib_left.at[distance - 1, b], sl_send.at[distance - 1, b],
-                    sl_recv.at[distance - 1, b], sibling,
-                )
-                blocks.append(src)
+                blocks.append(left_in.at[distance - 1, b])
             if (distance, b) in lefts:
-                lefts[distance, b].wait_recv()
-                send_left(distance + 1, b)
-                src = right_in.at[distance - 1, b]
-                sib_rights[distance, b] = send(
-                    src, sib_right.at[distance - 1, b], sr_send.at[distance - 1, b],
-                    sr_recv.at[distance - 1, b], sibling,
-                )
-                blocks.append(src)
+                blocks.append(right_in.at[distance - 1, b])
             if distance == 1:
                 sib_owns[b].wait_recv()
                 blocks.append(sib_own.at[b])
@@ -296,9 +295,19 @@
                         copies[distance - 1, b].wait_recv()
                         blocks.append(held.at[distance - 2, b])
             absorb(b, blocks)
-        if distance <= levels:
-            exchange(distance)
-    for level in range(half + 1, levels + 1):
+
+    exchange(1)
+    for distance in range(1, half + 1):
+        pass_on(distance)
+        if distance == 1:
+            for b in range(samples):
+                near(b)
+        else:
+            absorb_stage(distance - 1)
+        if distance + 1 <= levels:
+            exchange(distance + 1)
+    absorb_stage(half)
+    for level in range(half + 2, levels + 1):
         exchange(level)
     sums[...] = part[levels]
 

time: 32.5 us -> 34.4 us (1.058)
  Pallas kernels: 31.6 us -> 33.6 us
    pallas_call x1, Pallas kernels: 28.7 us -> 30.7 us  [per_device(): pl.pallas_call(functools.partial(attend_kernel, seq_count, natural), out_...]
where the time goes in v3:
time: 34.4 us; the launch traced here: 34.3 us
  Pallas kernels  33.6 us (98%)
  between operations  0.69 us (2%)
    pallas_call x1, Pallas kernels, per_device(): pl.pallas_call(functools.partial(attend_kernel, seq_count, natural), out_...  30.7 us
    pallas_call x1, Pallas kernels, per_device(): pl.pallas_call(functools.partial(finish_kernel, float(tokens * seq_count)...  2.89 us

profile of v3, /device:TPU:0, one launch (start us, length us, event | category | flops | bytes accessed | tf_op | source)
XLA Modules:
  0.0 34.3 jit_solution(13356917396522510543)
XLA Ops:
  0.6 0.0 copy-start
  0.6 0.0 copy-start.1
  0.7 0.0 copy-start.2
  0.7 30.7 %attend.1 = (bf16[256,384]{1,0:T(8,128)(2,1)S(1)}, f32[16,128]{1,0:T(8,128)S(1)}) custom-call(bf16[2,128,3072]{2,1,0:T(8,128)(2,1)} %images.1, bf16[3072,1152]{1,0:T(8,128)(2,1)} %w_qkv.1, f32[1152]{0:T(1024)} %b_qkv.1, f32[128]{0:T(128)} %q_gain.1, f32[128]{0:T(128)} %k_gain.1, f32[3,32,128]{2,1,0:T(8,128)} %bitcast.6, f32[3,32,128]{2,1,0:T(8,128)} %bitcast.7, ...), custom_call_target="tpu_custom_call" | custom-call | tf_op jit(solution)/shard_map/attend/pallas_call | solution.py:381
  31.4 0.0 copy-done
  31.4 0.0 copy-done.1
  31.4 0.0 copy-done.2
  31.4 2.9 %finish.1 = (bf16[2,128,3072]{2,1,0:T(8,128)(2,1)}, f32[2,3,2,128]{3,2,1,0:T(2,128)}) custom-call(s32[2,3]{1,0:T(2,128)S(1)} %copy-done.2, bf16[256,384]{1,0:T(8,128)(2,1)S(1)} %get-tuple-element.6.attended, bf16[384,3072]{1,0:T(8,128)(2,1)S(1)} %copy-done, f32[16,128]{1,0:T(8,128)S(1)} %get-tuple-element.7.sums, f32[2,3,2,128]{3,2,1,0:T(2,128)S(1)} %bitcast.5), custom_call_target="tpu_custom_call" | custom-call | tf_op jit(solution)/shard_map/finish/pallas_call | solution.py:431
Async XLA Ops:
  0.6 30.7 %copy-start = (bf16[384,3072]{1,0:T(8,128)(2,1)S(1)}, bf16[384,3072]{1,0:T(8,128)(2,1)}, u32[]{:S(2)}) copy-start(bf16[384,3072]{1,0:T(8,128)(2,1)} %w_out.1) | copy-start | bytes 7077892
  0.6 30.7 %copy-start.1 = (f32[2,2,3,128]{3,1,2,0:T(2,128)S(1)}, f32[2,2,3,128]{3,1,2,0:T(2,128)}, u32[]{:S(2)}) copy-start(f32[2,2,3,128]{3,1,2,0:T(2,128)} %param.17) | copy-start | bytes 18436
  0.7 30.7 %copy-start.2 = (s32[2,3]{1,0:T(2,128)S(1)}, s32[2,3]{1,0:T(2,128)}, u32[]{:S(2)}) copy-start(s32[2,3]{1,0:T(2,128)} %refresh.1) | copy-start | bytes 76

commit v4 on v2

--- a/solution.py
+++ b/solution.py
@@ -9,7 +9,7 @@
 from jax.sharding import PartitionSpec as P
 
 epsilon = 1e-06
-highest = lax.Precision.HIGHEST
+highest = lax.Precision.HIGH
 LANES = 128
 ROW_CHUNKS = 6
 OUT_TILES = 6
@@ -78,6 +78,12 @@
     for device in greeted:
         pl.semaphore_signal(barrier, inc=1, device_id={"seq": device}, device_id_type=MESH)
 
+    small = []
+    pairs = [(b_qkv, b_s), (q_gain, qg_s), (k_gain, kg_s), (key_basis, kb_s), (value_basis, vb_s), (centers, cen_s)]
+    for i, (src, dst) in enumerate(pairs):
+        c = pltpu.make_async_copy(src, dst, small_sem.at[i])
+        c.start()
+        small.append(c)
     step = width // ROW_CHUNKS
     img_copies, kv_copies = [], []
     for i in range(ROW_CHUNKS):
@@ -90,12 +96,6 @@
         )
         c.start()
         kv_copies.append(c)
-    small = []
-    pairs = [(b_qkv, b_s), (q_gain, qg_s), (k_gain, kg_s), (key_basis, kb_s), (value_basis, vb_s), (centers, cen_s)]
-    for i, (src, dst) in enumerate(pairs):
-        c = pltpu.make_async_copy(src, dst, small_sem.at[i])
-        c.start()
-        small.append(c)
     q_copy = pltpu.make_async_copy(
         w_qkv.at[:, pl.ds(0, side)], w_s.at[:, pl.ds(0, side)], in_sem.at[ROW_CHUNKS]
     )

time: 32.5 us -> 31.1 us (0.957)
  Pallas kernels: 31.6 us -> 30.2 us
    pallas_call x1, Pallas kernels: 28.7 us -> 27.3 us  [per_device(): pl.pallas_call(functools.partial(attend_kernel, seq_count, natural), out_...]
where the time goes in v4:
time: 31.1 us; the launch traced here: 30.9 us
  Pallas kernels  30.2 us (97%)
  between operations  0.69 us (2%)
    pallas_call x1, Pallas kernels, per_device(): pl.pallas_call(functools.partial(attend_kernel, seq_count, natural), out_...  27.3 us
    pallas_call x1, Pallas kernels, per_device(): pl.pallas_call(functools.partial(finish_kernel, float(tokens * seq_count)...  2.89 us

profile of v4, /device:TPU:0, one launch (start us, length us, event | category | flops | bytes accessed | tf_op | source)
XLA Modules:
  0.0 30.9 jit_solution(13917973981418906559)
XLA Ops:
  0.6 0.0 copy-start
  0.6 0.0 copy-start.1
  0.7 0.0 copy-start.2
  0.7 27.3 %attend.1 = (bf16[256,384]{1,0:T(8,128)(2,1)S(1)}, f32[16,128]{1,0:T(8,128)S(1)}) custom-call(bf16[2,128,3072]{2,1,0:T(8,128)(2,1)} %images.1, bf16[3072,1152]{1,0:T(8,128)(2,1)} %w_qkv.1, f32[1152]{0:T(1024)} %b_qkv.1, f32[128]{0:T(128)} %q_gain.1, f32[128]{0:T(128)} %k_gain.1, f32[3,32,128]{2,1,0:T(8,128)} %bitcast.6, f32[3,32,128]{2,1,0:T(8,128)} %bitcast.7, ...), custom_call_target="tpu_custom_call" | custom-call | tf_op jit(solution)/shard_map/attend/pallas_call | solution.py:372
  28.0 0.0 copy-done
  28.0 0.0 copy-done.1
  28.0 0.0 copy-done.2
  28.0 2.9 %finish.1 = (bf16[2,128,3072]{2,1,0:T(8,128)(2,1)}, f32[2,3,2,128]{3,2,1,0:T(2,128)}) custom-call(s32[2,3]{1,0:T(2,128)S(1)} %copy-done.2, bf16[256,384]{1,0:T(8,128)(2,1)S(1)} %get-tuple-element.6.attended, bf16[384,3072]{1,0:T(8,128)(2,1)S(1)} %copy-done, f32[16,128]{1,0:T(8,128)S(1)} %get-tuple-element.7.sums, f32[2,3,2,128]{3,2,1,0:T(2,128)S(1)} %bitcast.5), custom_call_target="tpu_custom_call" | custom-call | tf_op jit(solution)/shard_map/finish/pallas_call | solution.py:422
Async XLA Ops:
  0.6 27.4 %copy-start = (bf16[384,3072]{1,0:T(8,128)(2,1)S(1)}, bf16[384,3072]{1,0:T(8,128)(2,1)}, u32[]{:S(2)}) copy-start(bf16[384,3072]{1,0:T(8,128)(2,1)} %w_out.1) | copy-start | bytes 7077892
  0.6 27.4 %copy-start.1 = (f32[2,2,3,128]{3,1,2,0:T(2,128)S(1)}, f32[2,2,3,128]{3,1,2,0:T(2,128)}, u32[]{:S(2)}) copy-start(f32[2,2,3,128]{3,1,2,0:T(2,128)} %param.17) | copy-start | bytes 18436
  0.7 27.4 %copy-start.2 = (s32[2,3]{1,0:T(2,128)S(1)}, s32[2,3]{1,0:T(2,128)}, u32[]{:S(2)}) copy-start(s32[2,3]{1,0:T(2,128)} %refresh.1) | copy-start | bytes 76
